TPU v7x, 256 devices: a whole 4x4x8 slice. The times are simulated.
256 devices in a mesh: fsdp: 2 (over y_hi), dp: 32 (over x, z), owner: 4 (over y_lo, core).
Axes of the slice: x: 4, y: 4 (y_hi: 2, y_lo: 2; y = y_hi * 2 + y_lo), z: 8, core: 2. Of those that a mesh axis runs over, the one named last changes fastest.
Arguments:
- hidden: bfloat16 [256, 256, 4096], P(('fsdp', 'dp', 'owner')), may hold values from -6 to 6
- norm_gain: float32 [4096], replicated, may hold values from 0.1 to 1.9
- query_weight: bfloat16 [4096, 2048], P(('fsdp', 'dp')), may hold values from -0.09375 to 0.09375
- key_value_weight: bfloat16 [4096, 1024], P(('fsdp', 'dp')), may hold values from -0.09375 to 0.09375
- lengths: int32 [256], P(('fsdp', 'dp', 'owner')), may hold values from 128 to 256, as said below
- cotangent: bfloat16 [256, 256, 2048], P(('fsdp', 'dp', 'owner')), may hold values from -6 to 6
- cartridge: float32 [512, 1024], P('owner'), may hold values from -48 to 48
- adam_first_moment: float32 [512, 1024], P('owner'), may hold values from -6 to 6
- adam_second_moment: float32 [512, 1024], P('owner'), may hold values from 0.01 to 1
Outputs:
- attention_out: bfloat16 [256, 256, 2048], P(('fsdp', 'dp', 'owner'))
- new_cartridge: float32 [512, 1024], P('owner')
- new_first: float32 [512, 1024], P('owner')
- new_second: float32 [512, 1024], P('owner')
Inputs may be any that keep to these rules, and one draw needn't show every extreme that they name: `lengths`: each conversation's live tokens are its first rows; the rows after them are padding; some conversation is full.
All inputs are finite; a program needn't handle non-finite values.
Results may differ from a plain program's by a relative error of at most 0.008.
The roundings to bfloat16 on the way count: a program that leaves them out, or rounds other values in their place, can miss the bound.
Values may be sent and summed in bfloat16 or wider, within the bound.
No kernel may reach another device: no remote copies, remote signals or barrier semaphores. Data moves between devices by JAX's collectives and lax.ppermute only.
A program may use at most 128 MiB of HBM per device.

v0:
```python
import jax
import jax.numpy as jnp
from jax import lax
from jax.sharding import PartitionSpec as P

HEAD_SIZE = 128
QUERY_HEADS = 16
KEY_VALUE_HEADS = 4
STEP = 50


def rotary_heads(values, offset):
    sequence_rows = values.shape[0]
    half_size = values.shape[2] // 2
    exponent = jnp.arange(half_size, dtype=jnp.float32) * (2.0 / values.shape[2])
    inverse = jnp.power(jnp.float32(500000.0), -exponent)
    position = (offset + jnp.arange(sequence_rows)).astype(jnp.float32)
    angles = position[:, None] * inverse[None, :]
    cosine = jnp.cos(angles)[:, None, :]
    sine = jnp.sin(angles)[:, None, :]
    first_half = values[..., :half_size]
    second_half = values[..., half_size:]
    return jnp.concatenate(
        [first_half * cosine - second_half * sine, second_half * cosine + first_half * sine],
        axis=-1,
    )


def adam_update(current, moment_one, moment_two, prefix_gradient):
    one_new = 0.9 * moment_one + 0.1 * prefix_gradient
    two_new = 0.999 * moment_two + 0.001 * prefix_gradient * prefix_gradient
    one_fix = 1.0 - 0.9**STEP
    two_fix = 1.0 - 0.999**STEP
    updated = current - 0.02 * (one_new / one_fix) / (jnp.sqrt(two_new / two_fix) + 1e-08)
    return (updated, one_new, two_new)


def add_rows(pieces, features):
    return (
        jnp.dot(features, pieces[0], preferred_element_type=jnp.float32),
        jnp.dot(features, pieces[1], preferred_element_type=jnp.float32),
    )


def on_device(
    hidden,
    norm_gain,
    query_weight,
    key_value_weight,
    lengths,
    cotangent,
    cartridge,
    adam_first_moment,
    adam_second_moment,
):
    sequence_rows = hidden.shape[1]
    query_group_size = QUERY_HEADS // KEY_VALUE_HEADS
    score_scale = HEAD_SIZE ** (-0.5)
    states = hidden[0].astype(jnp.float32)
    normed = (
        states * lax.rsqrt(jnp.mean(states * states, axis=1, keepdims=True) + 1e-05) * norm_gain
    ).astype(jnp.bfloat16)
    proj_query, project_key_value = add_rows(
        (
            lax.all_gather(query_weight, ("fsdp", "dp"), axis=0, tiled=True),
            lax.all_gather(key_value_weight, ("fsdp", "dp"), axis=0, tiled=True),
        ),
        normed,
    )
    shard_rows = cartridge.shape[0]
    prefix_length = shard_rows * lax.axis_size("owner")
    query_rows = rotary_heads(
        proj_query.reshape(sequence_rows, QUERY_HEADS, HEAD_SIZE), prefix_length
    ).astype(jnp.bfloat16)
    sequence_keys = rotary_heads(
        project_key_value[:, : KEY_VALUE_HEADS * HEAD_SIZE].reshape(
            sequence_rows, KEY_VALUE_HEADS, HEAD_SIZE
        ),
        prefix_length,
    ).astype(jnp.bfloat16)
    sequence_values = (
        project_key_value[:, KEY_VALUE_HEADS * HEAD_SIZE :]
        .reshape(sequence_rows, KEY_VALUE_HEADS, HEAD_SIZE)
        .astype(jnp.bfloat16)
    )
    gathered_rows = lax.all_gather(cartridge.astype(jnp.bfloat16), "owner", axis=0, tiled=True)
    cartridge_keys = gathered_rows[:, : KEY_VALUE_HEADS * HEAD_SIZE].reshape(
        prefix_length, KEY_VALUE_HEADS, HEAD_SIZE
    )
    cartridge_values = gathered_rows[:, KEY_VALUE_HEADS * HEAD_SIZE :].reshape(
        prefix_length, KEY_VALUE_HEADS, HEAD_SIZE
    )
    grouped_heads = query_rows.reshape(sequence_rows, KEY_VALUE_HEADS, query_group_size, HEAD_SIZE)
    pre_scores = (
        jnp.einsum(
            "shgd,phd->hgsp", grouped_heads, cartridge_keys, preferred_element_type=jnp.float32
        )
        * score_scale
    )
    own_scores = (
        jnp.einsum(
            "shgd,thd->hgst", grouped_heads, sequence_keys, preferred_element_type=jnp.float32
        )
        * score_scale
    )
    causal = jnp.arange(sequence_rows)[:, None] >= jnp.arange(sequence_rows)[None, :]
    own_scores = jnp.where(causal, own_scores, -jnp.inf)
    highest = jnp.maximum(
        jnp.max(pre_scores, axis=-1, keepdims=True), jnp.max(own_scores, axis=-1, keepdims=True)
    )
    pre_exp = jnp.exp(pre_scores - highest)
    own_exp = jnp.exp(own_scores - highest)
    denominator = jnp.sum(pre_exp, axis=-1, keepdims=True) + jnp.sum(
        own_exp, axis=-1, keepdims=True
    )
    pre_probs = pre_exp / denominator
    pre_low = pre_probs.astype(jnp.bfloat16)
    own_low = (own_exp / denominator).astype(jnp.bfloat16)
    attended = jnp.einsum(
        "hgsp,phd->shgd", pre_low, cartridge_values, preferred_element_type=jnp.float32
    )
    attended = attended + jnp.einsum(
        "hgst,thd->shgd", own_low, sequence_values, preferred_element_type=jnp.float32
    )
    active_rows = (jnp.arange(sequence_rows) < lengths[0])[:, None, None, None]
    attention_out = jnp.where(active_rows, attended, 0.0).astype(jnp.bfloat16)
    upstream_gradient = jnp.where(
        active_rows,
        cotangent[0].reshape(sequence_rows, KEY_VALUE_HEADS, query_group_size, HEAD_SIZE),
        0.0,
    )
    delta = jnp.einsum(
        "shgd,shgd->hgs", upstream_gradient, attention_out, preferred_element_type=jnp.float32
    )
    dprob = jnp.einsum(
        "shgd,phd->hgsp", upstream_gradient, cartridge_values, preferred_element_type=jnp.float32
    )
    dscore = (pre_probs * (dprob - delta[..., None])).astype(jnp.bfloat16)
    gradient_keys = (
        jnp.einsum("hgsp,shgd->phd", dscore, grouped_heads, preferred_element_type=jnp.float32)
        * score_scale
    )
    gradient_values = jnp.einsum(
        "hgsp,shgd->phd", pre_low, upstream_gradient, preferred_element_type=jnp.float32
    )
    prefix_gradient = jnp.concatenate(
        [
            gradient_keys.reshape(prefix_length, KEY_VALUE_HEADS * HEAD_SIZE),
            gradient_values.reshape(prefix_length, KEY_VALUE_HEADS * HEAD_SIZE),
        ],
        axis=1,
    )
    summed = lax.psum(prefix_gradient, ("fsdp", "dp", "owner"))
    owned_sum = lax.dynamic_slice_in_dim(
        summed, lax.axis_index("owner") * shard_rows, shard_rows, 0
    )
    new_cartridge, new_first, new_second = adam_update(
        cartridge, adam_first_moment, adam_second_moment, owned_sum
    )
    return (
        attention_out.reshape(1, sequence_rows, QUERY_HEADS * HEAD_SIZE),
        new_cartridge,
        new_first,
        new_second,
    )


def solution(mesh):
    placed = (
        P(("fsdp", "dp", "owner"), None, None),
        P(),
        P(("fsdp", "dp"), None),
        P(("fsdp", "dp"), None),
        P(("fsdp", "dp", "owner")),
        P(("fsdp", "dp", "owner"), None, None),
        P("owner", None),
        P("owner", None),
        P("owner", None),
    )
    return jax.shard_map(
        on_device,
        mesh=mesh,
        in_specs=placed,
        out_specs=(
            P(("fsdp", "dp", "owner"), None, None),
            P("owner", None),
            P("owner", None),
            P("owner", None),
        ),
        check_vma=False,
    )
```

profile of v0, /device:TPU:2, one launch (start us, length us, event | category | flops | bytes accessed | tf_op | source)
XLA Modules:
  0.0 717.0 jit_solution(16635561501502723550)
XLA Ops:
  7.2 2.0 copy.31
  9.3 0.7 all-gather.8.cloned.1.call-update
  10.1 0.7 all-gather.4.cloned.1.call-update
  12.0 2.3 copy.39
  14.3 0.5 fusion.7
  14.8 21.3 %all-gather.6.cloned.1.call-done = bf16[512,1024]{0,1:T(8,128)(2,1)} async-done(((bf16[128,1024]{0,1:T(8,128)(2,1)}), bf16[512,1024]{0,1:T(8,128)(2,1)}) %all-gather.6.cloned.1.call-update) | async-done | bytes 1048592 | tf_op jit(solution)/shard_map/all_gather | solution.py:86
  36.1 2.1 fusion.62
  38.2 149.8 %all-gather.8.cloned.1.call-done = bf16[4096,1024]{1,0:T(8,128)(2,1)} async-done(((bf16[64,1024]{1,0:T(8,128)(2,1)}), bf16[4096,1024]{1,0:T(8,128)(2,1)}) %all-gather.8.cloned.1.call-update) | async-done | bytes 8388624 | tf_op jit(solution)/shard_map/all_gather | solution.py:66
  188.0 5.8 fusion.22
  194.1 0.8 copy.60
  194.9 0.3 fusion.63
  195.2 0.8 subtract_convert_fusion.1
  196.1 191.2 %all-gather.4.cloned.1.call-done = bf16[4096,2048]{1,0:T(8,128)(2,1)} async-done(((bf16[64,2048]{1,0:T(8,128)(2,1)}), bf16[4096,2048]{1,0:T(8,128)(2,1)}) %all-gather.4.cloned.1.call-update) | async-done | bytes 16777232 | tf_op jit(solution)/shard_map/all_gather | solution.py:65
  387.3 21.5 %copy.28 = bf16[2048,4096]{1,0:T(8,128)(2,1)} copy(bf16[2048,4096]{0,1:T(8,128)(2,1)} %bitcast.119) | data formatting | bytes 33554432 | tf_op jit(solution)/shard_map/dot_general | solution.py:40
  408.9 8.3 %fusion.20 = f32[256,16,128]{0,2,1:T(8,128)S(1)} fusion(bf16[16,128,4096]{2,1,0:T(8,128)(2,1)} %bitcast.120, bf16[1,256,4096]{2,1,0:T(8,128)(2,1)S(1)} %copy-done.2, f32[4096]{0:T(1024)S(1)} %copy-done.12, f32[256]{0:T(256)S(1)} %add_rsqrt_fusion), kind=kOutput, calls=%fused_computation.26 | convolution fusion | flops 4299161600 | bytes 20988928 | tf_op jit(solution)/shard_map/dot_general | solution.py:40
  417.2 0.3 subtract_convert_fusion
  417.5 0.5 copy.30
  418.0 0.5 copy.29
  418.5 1.5 bitcast_reduce_fusion
  420.1 1.4 fusion.18
  421.5 0.9 fusion.17
  422.4 2.2 fusion.4
  424.7 1.6 fusion.35
  426.3 3.5 fusion.27
  429.8 4.0 fusion.24
  433.8 8.9 %fusion.41 = f32[4,128,512]{2,1,0:T(8,128)} fusion(f32[4,4,256]{2,1,0:T(4,128)S(1)} %get-tuple-element.29, bf16[512,4,128,1]{0,2,3,1:T(8,128)(2,1)} %bitcast.130, bf16[256,4,4,128]{0,3,2,1:T(8,128)(2,1)S(1)} %bitcast.126, pred[256]{0:T(512)(128)(4,1)S(1)} %iota_compare_fusion.1, bf16[256,4,4,64]{3,0,2,1:T(8,128)(2,1)S(1)} %copy.30, ...), kind=kOutput, calls=%fused_computation.44 | convolution fusion | flops 1089208320 | bytes 12108032 | tf_op jit(solution)/shard_map/hgsp,shgd->phd/dot_general | solution.py:140
  442.7 1.6 copy.42
  444.2 1.6 copy.41
  445.8 1.5 pad_maximum_fusion
  447.3 2.3 copy.43
  449.7 258.4 %all-reduce.2.cloned.1.call-done = f32[512,1024]{1,0:T(8,128)} async-done(((f32[512,1024]{1,0:T(8,128)}), f32[512,1024]{1,0:T(8,128)}) %all-reduce.2.cloned.1.call-update) | async-done | bytes 2097168 | tf_op jit(solution)/shard_map/psum | solution.py:153
  708.0 2.4 divide_subtract_fusion
  (45 shorter events, 1.1 us)
Async XLA Ops:
  7.2 7.1 copy-start.1
  7.2 180.8 %copy-start.12 = (f32[4096]{0:T(1024)S(1)}, f32[4096]{0:T(1024)}, u32[]{:S(2)}) copy-start(f32[4096]{0:T(1024)} %param.10) | copy-start | bytes 49156
  7.2 29.0 %all-gather.6.cloned.1.call-start = ((), (), s32[]{:S(2)}) async-start(), calls=%async_computation.1 | async-start | bytes 1310720 | tf_op jit(solution)/shard_map/all_gather | solution.py:86
  9.3 178.7 %all-gather.8.cloned.1.call-start = ((), (), s32[]{:S(2)}) async-start(), calls=%async_computation.2 | async-start | bytes 8519680 | tf_op jit(solution)/shard_map/all_gather | solution.py:66
  10.0 377.3 %all-gather.4.cloned.1.call-start = ((), (), s32[]{:S(2)}) async-start(), calls=%async_computation | async-start | bytes 17039360 | tf_op jit(solution)/shard_map/all_gather | solution.py:65
  10.8 697.3 %all-reduce.2.cloned.1.call-start = ((), (), s32[]{:S(2)}) async-start(), calls=%async_computation.3 | async-start | bytes 4194304 | tf_op jit(solution)/shard_map/psum | solution.py:153
  11.8 3.0 copy-start.6
  387.3 21.6 %copy-start.2 = (bf16[1,256,4096]{2,1,0:T(8,128)(2,1)S(1)}, bf16[1,256,4096]{2,1,0:T(8,128)(2,1)}, u32[]{:S(2)}) copy-start(bf16[1,256,4096]{2,1,0:T(8,128)(2,1)} %param.9) | copy-start | bytes 6291460
  408.9 8.4 %copy-start.7 = (f32[256,64]{0,1:T(8,128)S(1)}, f32[256,64]{0,1:T(8,128)}, u32[]{:S(2)}) copy-start(f32[256,64]{0,1:T(8,128)} %copy-done.6) | copy-start | bytes 196612
  418.5 1.6 copy-start.5
  420.1 9.7 %copy-start = (f32[4,256,4,512]{3,1,2,0:T(8,128)}, f32[4,256,4,512]{3,1,2,0:T(8,128)S(1)}, u32[]{:S(2)}) copy-start(f32[4,256,4,512]{3,1,2,0:T(8,128)S(1)} %get-tuple-element.26) | copy-start | bytes 25165828
  422.4 2.2 copy-start.11
  424.6 1.6 copy-start.4
  426.3 3.5 copy-start.10
  445.8 262.2 %copy-start.3 = (f32[128,1024]{1,0:T(8,128)S(1)}, f32[128,1024]{1,0:T(8,128)}, u32[]{:S(2)}) copy-start(f32[128,1024]{1,0:T(8,128)} %param.15) | copy-start | bytes 1572868
  445.8 262.2 %copy-start.8 = (f32[128,1024]{1,0:T(8,128)S(1)}, f32[128,1024]{1,0:T(8,128)}, u32[]{:S(2)}) copy-start(f32[128,1024]{1,0:T(8,128)} %param.16) | copy-start | bytes 1572868
  447.3 260.7 %copy-start.9 = (f32[128,1024]{1,0:T(8,128)S(1)}, f32[128,1024]{1,0:T(8,128)}, u32[]{:S(2)}) copy-start(f32[128,1024]{1,0:T(8,128)} %param.17) | copy-start | bytes 1572868
Sparse Core Ops, SparseCore 0:
  10.4 25.7 all-gather.5
  39.8 148.1 all-gather.7
  191.7 195.5 all-gather.3
  447.5 260.5 all-reduce.1
where the time goes:
time: 718 us; the launch traced here: 717 us
  waiting for transfers between devices  622 us (87%)
  local copies, waits for them, and re-layouts  36 us (5%)
  matrix products  35 us (5%)
  between operations  14.7 us (2%)
  other arithmetic  9.01 us (1%)
    psum x1, waiting for transfers between devices, on_device(): summed = lax.psum(prefix_gradient, ('fsdp', 'dp', 'owner'))  258 us
    all_gather x1, waiting for transfers between devices, on_device(): lax.all_gather(query_weight, ('fsdp', 'dp'), axis=0, tiled=True)  191 us
    all_gather x1, waiting for transfers between devices, on_device(): lax.all_gather(key_value_weight, ('fsdp', 'dp'), axis=0, tiled=True)  150 us
    dot_general x1, local copies, waits for them, and re-layouts, add_rows(): jnp.dot(features, pieces[0], preferred_element_type=jnp.float32)  21.5 us
    all_gather x1, waiting for transfers between devices, on_device(): lax.all_gather(cartridge.astype(jnp.bfloat16), 'owner', axis=0, tiled=True)  21.3 us
  transfers between devices with their start and end apart: 4, of which 4 were waited for; matrix products, arithmetic and copies ran while one was open for 2% of the time, Pallas kernels for 0%

commit v1 on v0

--- a/solution.py
+++ b/solution.py
@@ -150,7 +150,7 @@
         ],
         axis=1,
     )
-    summed = lax.psum(prefix_gradient, ("fsdp", "dp", "owner"))
+    summed = jax.lax.psum(jax.lax.psum(prefix_gradient, "fsdp"), ("dp", "owner"))
     owned_sum = lax.dynamic_slice_in_dim(
         summed, lax.axis_index("owner") * shard_rows, shard_rows, 0
     )

time: 718 us -> 1630 us (2.27)
  the two profiles are of different devices: /device:TPU:2 before, /device:TPU:16 now
where the time goes in v1:
time: 1630 us
  waiting for transfers between devices  1540 us (94%)
  matrix products  35.1 us (2%)
  local copies, waits for them, and re-layouts  34.4 us (2%)
    psum x1, waiting for transfers between devices, on_device(): jax.lax.psum(jax.lax.psum(prefix_gradient, 'fsdp'), ('dp', 'owner'))  1100 us
    all_gather x1, waiting for transfers between devices, on_device(): lax.all_gather(query_weight, ('fsdp', 'dp'), axis=0, tiled=True)  191 us
    all_gather x1, waiting for transfers between devices, on_device(): lax.all_gather(key_value_weight, ('fsdp', 'dp'), axis=0, tiled=True)  147 us
    psum x1, waiting for transfers between devices, on_device(): jax.lax.psum(prefix_gradient, 'fsdp')  72.9 us
  transfers between devices with their start and end apart: 5, of which 5 were waited for; matrix products, arithmetic and copies ran while one was open for 1% of the time, Pallas kernels for 0%

profile of v1, /device:TPU:16, one launch (start us, length us, event | category | flops | bytes accessed | tf_op | source)
XLA Modules:
  0.0 1632.2 jit_solution(17208073496898405009)
XLA Ops:
  7.2 2.0 copy.31
  9.3 0.7 all-gather.8.cloned.1.call-update
  10.1 0.7 all-gather.4.cloned.1.call-update
  12.0 2.3 copy.39
  14.3 0.5 fusion.7
  14.8 21.2 %all-gather.6.cloned.1.call-done = bf16[512,1024]{0,1:T(8,128)(2,1)} async-done(((bf16[128,1024]{0,1:T(8,128)(2,1)}), bf16[512,1024]{0,1:T(8,128)(2,1)}) %all-gather.6.cloned.1.call-update) | async-done | bytes 1048592 | tf_op jit(solution)/shard_map/all_gather | solution.py:86
  36.0 2.1 fusion.62
  38.0 147.3 %all-gather.8.cloned.1.call-done = bf16[4096,1024]{1,0:T(8,128)(2,1)} async-done(((bf16[64,1024]{1,0:T(8,128)(2,1)}), bf16[4096,1024]{1,0:T(8,128)(2,1)}) %all-gather.8.cloned.1.call-update) | async-done | bytes 8388624 | tf_op jit(solution)/shard_map/all_gather | solution.py:66
  185.4 5.8 fusion.22
  191.4 0.8 copy.60
  192.2 0.3 fusion.63
  192.6 0.8 subtract_convert_fusion.1
  193.4 191.2 %all-gather.4.cloned.1.call-done = bf16[4096,2048]{1,0:T(8,128)(2,1)} async-done(((bf16[64,2048]{1,0:T(8,128)(2,1)}), bf16[4096,2048]{1,0:T(8,128)(2,1)}) %all-gather.4.cloned.1.call-update) | async-done | bytes 16777232 | tf_op jit(solution)/shard_map/all_gather | solution.py:65
  384.6 20.9 %copy.28 = bf16[2048,4096]{1,0:T(8,128)(2,1)} copy(bf16[2048,4096]{0,1:T(8,128)(2,1)} %bitcast.119) | data formatting | bytes 33554432 | tf_op jit(solution)/shard_map/dot_general | solution.py:40
  405.5 8.3 fusion.20
  414.2 0.5 copy.30
  414.7 0.5 copy.29
  415.2 1.5 bitcast_reduce_fusion
  416.7 1.4 fusion.18
  418.2 0.9 fusion.17
  419.1 2.2 fusion.4
  421.3 1.6 fusion.35
  423.0 3.5 fusion.27
  426.5 4.0 fusion.24
  430.4 8.9 fusion.41
  439.4 1.6 copy.42
  440.9 1.6 copy.41
  442.5 1.5 pad_maximum_fusion
  444.1 72.9 %all-reduce.3.cloned.1.call-done = f32[512,1024]{1,0:T(8,128)} async-done(((f32[512,1024]{1,0:T(8,128)}), f32[512,1024]{1,0:T(8,128)}) %all-reduce.3.cloned.1.call-update) | async-done | bytes 2097168 | tf_op jit(solution)/shard_map/psum | solution.py:153
  517.0 1.4 copy.43
  518.4 1104.9 %all-reduce.5.cloned.1.call-done = f32[512,1024]{1,0:T(8,128)} async-done(((f32[512,1024]{1,0:T(8,128)}), f32[512,1024]{1,0:T(8,128)}) %all-reduce.5.cloned.1.call-update) | async-done | bytes 2097168 | tf_op jit(solution)/shard_map/psum | solution.py:153
  1623.3 2.4 divide_subtract_fusion
  (50 shorter events, 1.4 us)
Async XLA Ops:
  7.2 7.1 copy-start.1
  7.2 178.2 %copy-start.13 = (f32[4096]{0:T(1024)S(1)}, f32[4096]{0:T(1024)}, u32[]{:S(2)}) copy-start(f32[4096]{0:T(1024)} %param.10) | copy-start | bytes 49156
  7.2 28.8 %all-gather.6.cloned.1.call-start = ((), (), s32[]{:S(2)}) async-start(), calls=%async_computation.1 | async-start | bytes 1310720 | tf_op jit(solution)/shard_map/all_gather | solution.py:86
  9.3 176.1 %all-gather.8.cloned.1.call-start = ((), (), s32[]{:S(2)}) async-start(), calls=%async_computation.2 | async-start | bytes 8519680 | tf_op jit(solution)/shard_map/all_gather | solution.py:66
  10.0 374.6 %all-gather.4.cloned.1.call-start = ((), (), s32[]{:S(2)}) async-start(), calls=%async_computation | async-start | bytes 17039360 | tf_op jit(solution)/shard_map/all_gather | solution.py:65
  10.8 506.2 %all-reduce.3.cloned.1.call-start = ((), (), s32[]{:S(2)}) async-start(), calls=%async_computation.3 | async-start | bytes 4194304 | tf_op jit(solution)/shard_map/psum | solution.py:153
  11.8 3.0 copy-start.7
  384.6 20.9 %copy-start.2 = (bf16[1,256,4096]{2,1,0:T(8,128)(2,1)S(1)}, bf16[1,256,4096]{2,1,0:T(8,128)(2,1)}, u32[]{:S(2)}) copy-start(bf16[1,256,4096]{2,1,0:T(8,128)(2,1)} %param.9) | copy-start | bytes 6291460
  405.5 8.4 copy-start.8
  415.2 1.6 copy-start.6
  416.7 9.7 copy-start
  419.1 2.2 copy-start.12
  421.3 1.6 copy-start.4
  423.0 3.5 copy-start.11
  442.5 74.5 %copy-start.5 = (bf16[256,4,4,128]{0,3,2,1:T(8,128)(2,1)S(1)}, bf16[256,4,4,128]{0,3,2,1:T(8,128)(2,1)}, u32[]{:S(2)}) copy-start(bf16[256,4,4,128]{0,3,2,1:T(8,128)(2,1)} %get-tuple-element.30) | copy-start | bytes 3145732
  444.0 1179.3 %copy-start.3 = (f32[128,1024]{1,0:T(8,128)S(1)}, f32[128,1024]{1,0:T(8,128)}, u32[]{:S(2)}) copy-start(f32[128,1024]{1,0:T(8,128)} %param.15) | copy-start | bytes 1572868
  444.0 1179.3 %copy-start.9 = (f32[128,1024]{1,0:T(8,128)S(1)}, f32[128,1024]{1,0:T(8,128)}, u32[]{:S(2)}) copy-start(f32[128,1024]{1,0:T(8,128)} %param.16) | copy-start | bytes 1572868
  444.0 1179.3 %copy-start.10 = (f32[128,1024]{1,0:T(8,128)S(1)}, f32[128,1024]{1,0:T(8,128)}, u32[]{:S(2)}) copy-start(f32[128,1024]{1,0:T(8,128)} %param.17) | copy-start | bytes 1572868
  444.0 1179.3 %all-reduce.5.cloned.1.call-start = ((), (), s32[]{:S(2)}) async-start(), calls=%async_computation.4 | async-start | bytes 4194304 | tf_op jit(solution)/shard_map/psum | solution.py:153
Sparse Core Ops, SparseCore 0:
  10.4 25.5 all-gather.5
  39.6 145.6 all-gather.7
  189.0 195.5 all-gather.3
  444.2 72.7 all-reduce.2
  519.4 1103.8 all-reduce.4
